TPU v7x, 32 devices: a whole 2x2x4 slice. The times are simulated.
32 devices in a mesh: dp: 4 (over y, x), psg: 8 (over z, core).
Axes of the slice: x: 2, y: 2, z: 4, core: 2. Of those that a mesh axis runs over, the one named last changes fastest.
Arguments:
- queries: bfloat16 [4, 128, 2048], P('dp', None, 'psg'), may hold values from -4 to 4
- keys: bfloat16 [4, 16, 256, 2048], P('dp', 'psg'), may hold values from -4 to 4
- values: bfloat16 [4, 16, 256, 2048], P('dp', 'psg'), may hold values from -6 to 6
- lengths: int32 [4, 16], P('dp', 'psg'), may hold values from 16 to 256, as said below
- out_weight: bfloat16 [4096, 2048], P('psg'), may hold values from -0.125 to 0.125
- out_cotangent: bfloat16 [4, 128, 4096], P('dp', None, 'psg'), may hold values from -6 to 6
Outputs:
- layer_out: bfloat16 [4, 128, 4096], P('dp', None, 'psg')
- weight_grad: float32 [4096, 2048], P('psg')
- query_grad: bfloat16 [4, 128, 2048], P('dp', None, 'psg')
- key_grad: bfloat16 [4, 16, 256, 2048], P('dp', 'psg')
- value_grad: bfloat16 [4, 16, 256, 2048], P('dp', 'psg')
Inputs may be any that keep to these rules, and one draw needn't show every extreme that they name: `lengths`: every passage has at least 16 valid tokens, counted from its start; in every question some passage has all 256.
All inputs are finite; a program needn't handle non-finite values.
Results may differ from a plain program's by a relative error of at most 0.025.
Values may be sent and summed in bfloat16 or wider, within the bound.
No kernel may reach another device: no remote copies, remote signals or barrier semaphores. Data moves between devices by JAX's collectives and lax.ppermute only.
A program may use at most 64 MiB of HBM per device.

v0:
```python
import jax
import jax.numpy as jnp
from jax import lax
from jax.sharding import PartitionSpec as P

HEAD_COUNT = 32
HEAD_SIZE = 64


def spread_heads(factor):
    return jnp.transpose(factor, (0, 2, 1))[..., None]


def local_weights(scores, valid_keys, row_max):
    return jnp.where(valid_keys, jnp.exp(scores - row_max[..., None]), 0.0)


def weighted_values(weights, value_heads):
    output = jnp.einsum(
        "bhik,bkhe->bihe",
        weights.astype(jnp.bfloat16),
        value_heads,
        preferred_element_type=jnp.float32,
    )
    return output.reshape(output.shape[0], output.shape[1], -1)


def per_device(queries, keys, values, lengths, out_weight, out_cotangent):
    question_count = keys.shape[0]
    key_count = keys.shape[1] * keys.shape[2]
    inner_dim = keys.shape[3]
    answer_len = queries.shape[1]
    head_split = (question_count, answer_len, HEAD_COUNT, HEAD_SIZE)
    query_full = lax.all_gather(queries, "psg", axis=2, tiled=True)
    query_heads = query_full.reshape(head_split)
    key_heads = keys.reshape(question_count, key_count, HEAD_COUNT, HEAD_SIZE)
    value_heads = values.reshape(question_count, key_count, HEAD_COUNT, HEAD_SIZE)
    positions = jnp.arange(keys.shape[2], dtype=jnp.int32)
    valid_keys = (positions[None, None, :] < lengths[:, :, None]).reshape(
        question_count, 1, 1, key_count
    )
    scores = jnp.einsum(
        "bihe,bkhe->bhik", query_heads, key_heads, preferred_element_type=jnp.float32
    )
    local_max = jnp.max(jnp.where(valid_keys, scores, -jnp.inf), axis=3)
    row_max = lax.pmax(local_max, "psg")
    weights = local_weights(scores, valid_keys, row_max)
    row_sum, output = lax.psum(
        (jnp.sum(weights, axis=3), weighted_values(weights, value_heads)), "psg"
    )
    context = (
        (output.reshape(head_split) / spread_heads(row_sum))
        .astype(jnp.bfloat16)
        .reshape(question_count, answer_len, inner_dim)
    )
    context_rows = context.reshape(question_count * answer_len, inner_dim)
    grad_rows = out_cotangent.reshape(question_count * answer_len, -1)
    layer_out = jnp.dot(context_rows, out_weight.T, preferred_element_type=jnp.float32).astype(
        jnp.bfloat16
    )
    layer_out = layer_out.reshape(question_count, answer_len, -1)
    weight_grad = lax.psum(
        jnp.dot(grad_rows.T, context_rows, preferred_element_type=jnp.float32).astype(jnp.bfloat16),
        "dp",
    ).astype(jnp.float32)
    context_grad = lax.psum(
        jnp.dot(grad_rows, out_weight, preferred_element_type=jnp.float32), "psg"
    ).astype(jnp.bfloat16)
    grad_heads = context_grad.reshape(head_split)
    products = context_grad.reshape(question_count, answer_len, inner_dim).astype(
        jnp.float32
    ) * context.astype(jnp.float32)
    row_dots = jnp.transpose(jnp.sum(products.reshape(head_split), axis=3), (0, 2, 1))
    probs = weights / row_sum[..., None]
    prob_grad = jnp.einsum(
        "bihe,bkhe->bhik", grad_heads, value_heads, preferred_element_type=jnp.float32
    )
    score_grad = (probs * (prob_grad - row_dots[..., None])).astype(jnp.bfloat16)
    value_grad = jnp.einsum(
        "bhik,bihe->bkhe",
        probs.astype(jnp.bfloat16),
        grad_heads,
        preferred_element_type=jnp.float32,
    )
    value_grad = value_grad.astype(jnp.bfloat16).reshape(values.shape)
    key_grad = jnp.einsum(
        "bhik,bihe->bkhe", score_grad, query_heads, preferred_element_type=jnp.float32
    )
    key_grad = key_grad.astype(jnp.bfloat16).reshape(keys.shape)
    query_terms = jnp.einsum(
        "bhik,bkhe->bihe", score_grad, key_heads, preferred_element_type=jnp.float32
    )
    query_terms = query_terms.reshape(question_count, answer_len, inner_dim)
    query_grad = lax.psum_scatter(query_terms, "psg", scatter_dimension=2, tiled=True).astype(
        jnp.bfloat16
    )
    return (layer_out, weight_grad, query_grad, key_grad, value_grad)


def solution(mesh):
    return jax.shard_map(
        per_device,
        mesh=mesh,
        in_specs=(
            P("dp", None, "psg"),
            P("dp", "psg", None, None),
            P("dp", "psg", None, None),
            P("dp", "psg"),
            P("psg", None),
            P("dp", None, "psg"),
        ),
        out_specs=(
            P("dp", None, "psg"),
            P("psg", None),
            P("dp", None, "psg"),
            P("dp", "psg", None, None),
            P("dp", "psg", None, None),
        ),
        check_vma=False,
    )
```

profile of v0, /device:TPU:0, one launch (start us, length us, event | category | flops | bytes accessed | tf_op | source)
XLA Modules:
  0.0 291.0 jit_solution(12191987388623553962)
XLA Ops:
  7.2 16.8 %all_gather.3 = bf16[1,128,2048]{2,1,0:T(8,128)(2,1)S(1)} all-gather(bf16[1,128,256]{2,1,0:T(8,128)(2,1)} %param.6), channel_id=1, replica_groups=mesh['dp'=4,'psg'=8] {'psg'}, dimensions={2}, use_global_device_ids=true | all-gather | bytes 589824 | tf_op jit(solution)/shard_map/all_gather | solution.py:34
  24.4 6.3 %copy.25 = bf16[1,2,256,2048]{2,1,3,0:T(2,128)(2,1)} copy(bf16[1,2,256,2048]{3,2,1,0:T(8,128)(2,1)} %param.7) | data formatting | bytes 4194304 | tf_op args[1]
  30.7 4.4 %reshape.146 = bf16[512,32,64]{0,2,1:T(8,128)(2,1)} reshape(bf16[1,2,256,2048]{2,1,3,0:T(2,128)(2,1)} %copy.25) | data formatting | bytes 4194304 | tf_op jit(solution)/shard_map/reshape.4
  35.1 6.1 %copy.26 = bf16[1,2,256,2048]{2,1,3,0:T(2,128)(2,1)} copy(bf16[1,2,256,2048]{3,2,1,0:T(8,128)(2,1)} %param.8) | data formatting | bytes 4194304 | tf_op args[2]
  41.2 4.4 %reshape.147 = bf16[512,32,64]{0,2,1:T(8,128)(2,1)} reshape(bf16[1,2,256,2048]{2,1,3,0:T(2,128)(2,1)} %copy.26) | data formatting | bytes 4194304 | tf_op jit(solution)/shard_map/reshape.10
  45.7 6.1 %select_reduce_fusion = (f32[32,128]{1,0:T(8,128)S(1)}, f32[32,128,512]{2,1,0:T(8,128)}) fusion(pred[512]{0:T(512)(128)(4,1)S(1)} %lt.27, bf16[128,32,64]{0,2,1:T(8,128)(2,1)S(1)} %bitcast.89, bf16[512,32,64]{0,2,1:T(8,128)(2,1)} %reshape.146), kind=kOutput, calls=%fused_computation.2 | convolution fusion | flops 272625664 | bytes 11026944 | tf_op jit(solution)/shard_map/bihe,bkhe->bhik/dot_general | solution.py:42
  51.8 29.1 %pmax.7 = f32[32,128]{1,0:T(8,128)S(1)} all-reduce(f32[32,128]{1,0:T(8,128)S(1)} %get-tuple-element.19), channel_id=1, replica_groups=mesh['dp'=4,'psg'=8] {'psg'}, use_global_device_ids=true, to_apply=%region_1.2 | all-reduce | flops 4096 | bytes 32768 | tf_op jit(solution)/shard_map/pmax | solution.py:46
  81.0 5.7 %fusion.3 = f32[32,128,64]{1,2,0:T(8,128)S(1)} fusion(bf16[512,32,64]{0,2,1:T(8,128)(2,1)} %reshape.147, f32[32,128,512]{2,1,0:T(8,128)} %get-tuple-element.20, f32[32,128]{1,0:T(8,128)S(1)} %pmax.7, pred[512]{0:T(512)(128)(4,1)S(1)} %lt.27), kind=kOutput, calls=%fused_computation.6 | convolution fusion | flops 274726912 | bytes 11551232 | tf_op jit(solution)/shard_map/bhik,bkhe->bihe/dot_general | solution.py:19
  86.7 1.4 copy.27
  88.2 0.4 fusion.17
  88.6 4.6 %fusion.1 = f32[32,128]{1,0:T(8,128)S(1)} fusion(f32[32,128,512]{2,1,0:T(8,128)} %get-tuple-element.20, f32[32,128]{1,0:T(8,128)S(1)} %pmax.7, pred[512]{0:T(512)(128)(4,1)S(1)} %lt.27), kind=kLoop, calls=%fused_computation.4 | loop fusion | flops 6287360 | bytes 8421888 | tf_op jit(solution)/shard_map/reduce_sum | solution.py:49
  93.3 61.3 %all-reduce.8 = (f32[1,32,128]{2,1,0:T(8,128)S(1)}, bf16[128,2048]{1,0:T(8,128)(2,1)}) all-reduce(f32[1,32,128]{2,1,0:T(8,128)S(1)} %bitcast.95, f32[128,2048]{1,0:T(8,128)S(1)} %fusion.17), channel_id=1, replica_groups=mesh['dp'=4,'psg'=8] {'psg'}, use_global_device_ids=true, to_apply=%region_4.5 | all-reduce | flops 266240 | bytes 1605632 | tf_op jit(solution)/shard_map/psum | solution.py:48
  154.5 2.1 copy.30
  156.7 1.3 copy.28
  158.0 3.1 %convert_multiply_fusion = (f32[128,2048]{1,0:T(8,128)}, bf16[128,2048]{1,0:T(8,128)(2,1)}) fusion(bf16[128,2048]{1,0:T(8,128)(2,1)} %get-tuple-element.16, f32[128,2048]{1,0:T(8,128)} %copy.28, f32[1,128,2048]{2,1,0:T(8,128)} %all-reduce.5.cloned.1.call-done), kind=kLoop, calls=%fused_computation.21 | loop fusion | flops 1310720 | bytes 4194304 | tf_op jit(solution)/shard_map/mul | solution.py:70
  161.0 2.6 copy.31
  163.7 1.3 bitcast_reduce_fusion
  165.0 5.9 %multiply_convert_fusion = bf16[32,128,512]{2,1,0:T(8,128)(2,1)S(1)} fusion(f32[32,128]{1,0:T(8,128)S(1)} %bitcast.99, bf16[128,32,64]{0,2,1:T(8,128)(2,1)} %bitcast.93, bf16[512,32,64]{0,2,1:T(8,128)(2,1)} %reshape.147, f32[32,128]{1,0:T(8,128)S(1)} %bitcast.97, f32[32,128,512]{2,1,0:T(8,128)} %get-tuple-element.20, f32[32,128]{1,0:T(8,128)S(1)} %pmax.7, ...), kind=kOutput, calls=%fused_computation | convolution fusion | flops 281018368 | bytes 15254016 | tf_op jit(solution)/shard_map/bihe,bkhe->bhik/dot_general | solution.py:75
  170.9 2.5 fusion.23
  173.4 2.6 copy.32
  176.3 1.3 copy.29
  177.6 3.7 %fusion.10 = bf16[512,2048]{0,1:T(8,128)(2,1)} fusion(f32[1,128,2048]{2,1,0:T(8,128)} %all-reduce.5.cloned.1.call-done, f32[1,128,2048]{2,1,0:T(8,128)} %copy.29, bf16[1,128,512]{2,1,0:T(8,128)(2,1)S(1)} %copy-done.7), kind=kOutput, calls=%fused_computation.13 | convolution fusion | flops 270008320 | bytes 4325376 | tf_op jit(solution)/shard_map/dot_general | solution.py:63
  181.4 5.8 %convert_bitcast_fusion = bf16[1,512,32,64]{1,3,2,0:T(8,128)(2,1)} fusion(bf16[128,32,64]{0,2,1:T(8,128)(2,1)S(1)} %bitcast.94, f32[32,128]{1,0:T(8,128)S(1)} %bitcast.98, f32[32,128,512]{2,1,0:T(8,128)} %get-tuple-element.20, f32[32,128]{1,0:T(8,128)S(1)} %pmax.7, pred[512]{0:T(512)(128)(4,1)S(1)} %lt.27), kind=kOutput, calls=%fused_computation.14 | convolution fusion | flops 277872640 | bytes 11043328 | tf_op jit(solution)/shard_map/bhik,bihe->bkhe/dot_general | solution.py:79
  187.1 4.0 %reshape.156 = bf16[1,2,256,2048]{2,1,3,0:T(2,128)(2,1)} reshape(bf16[1,512,32,64]{1,3,2,0:T(8,128)(2,1)} %convert_bitcast_fusion) | data formatting | bytes 4194304 | tf_op jit(solution)/shard_map/reshape | solution.py:85
  191.2 6.1 %copy.35 = bf16[1,2,256,2048]{3,2,1,0:T(8,128)(2,1)} copy(bf16[1,2,256,2048]{2,1,3,0:T(2,128)(2,1)} %reshape.156) | data formatting | bytes 4194304
  197.3 4.2 %convert_bitcast_fusion.1 = bf16[1,512,32,64]{1,3,2,0:T(8,128)(2,1)} fusion(bf16[128,32,64]{0,2,1:T(8,128)(2,1)S(1)} %bitcast.90, bf16[32,128,512]{2,1,0:T(8,128)(2,1)} %copy-done.2), kind=kOutput, calls=%fused_computation.15 | convolution fusion | flops 269484032 | bytes 6815744 | tf_op jit(solution)/shard_map/bhik,bihe->bkhe/dot_general | solution.py:86
  201.6 4.0 %reshape.155 = bf16[1,2,256,2048]{2,1,3,0:T(2,128)(2,1)} reshape(bf16[1,512,32,64]{1,3,2,0:T(8,128)(2,1)} %convert_bitcast_fusion.1) | data formatting | bytes 4194304 | tf_op jit(solution)/shard_map/reshape | solution.py:89
  205.6 6.1 %copy.34 = bf16[1,2,256,2048]{3,2,1,0:T(8,128)(2,1)} copy(bf16[1,2,256,2048]{2,1,3,0:T(2,128)(2,1)} %reshape.155) | data formatting | bytes 4194304
  211.7 1.5 fusion.14
  213.2 1.5 convert_element_type.83
  214.8 65.7 %all-reduce.7.cloned.1.call-done = bf16[512,2048]{0,1:T(8,128)(2,1)} async-done(((bf16[512,2048]{0,1:T(8,128)(2,1)}), bf16[512,2048]{0,1:T(8,128)(2,1)}) %all-reduce.7.cloned.1.call-update) | async-done | bytes 2097168 | tf_op jit(solution)/shard_map/psum | solution.py:62
  280.4 4.1 %copy.33 = f32[512,2048]{1,0:T(8,128)} copy(bf16[512,2048]{0,1:T(8,128)(2,1)} %all-reduce.7.cloned.1.call-done) | data formatting | bytes 6291456
  (32 shorter events, 0.8 us)
Async XLA Ops:
  7.2 81.0 %copy-start = (bf16[512,2048]{1,0:T(8,128)(2,1)S(1)}, bf16[512,2048]{1,0:T(8,128)(2,1)}, u32[]{:S(2)}) copy-start(bf16[512,2048]{1,0:T(8,128)(2,1)} %param.10) | copy-start | bytes 6291460
  7.2 150.8 %all-reduce.5.cloned.1.call-start = ((), (), s32[]{:S(2)}) async-start(), calls=%async_computation.1 | async-start | bytes 2097152 | tf_op jit(solution)/shard_map/psum | solution.py:48
  24.4 21.3 %copy-start.3 = (bf16[1,128,2048]{1,2,0:T(8,128)(2,1)}, bf16[1,128,2048]{1,2,0:T(8,128)(2,1)S(1)}, u32[]{:S(2)}) copy-start(bf16[1,128,2048]{1,2,0:T(8,128)(2,1)S(1)} %copy.24) | copy-start | bytes 1572868
  35.1 10.5 %copy-start.8 = (s32[1,2]{1,0:T(1,128)S(1)}, s32[1,2]{1,0:T(1,128)}, u32[]{:S(2)}) copy-start(s32[1,2]{1,0:T(1,128)} %param.9) | copy-start | bytes 28
  80.9 7.2 %copy-start.7 = (bf16[1,128,512]{2,1,0:T(8,128)(2,1)S(1)}, bf16[1,128,512]{2,1,0:T(8,128)(2,1)}, u32[]{:S(2)}) copy-start(bf16[1,128,512]{2,1,0:T(8,128)(2,1)} %param.11) | copy-start | bytes 393220
  88.1 125.1 %reduce-scatter.2.cloned.1.call-start = ((), (), s32[]{:S(2)}) async-start(), calls=%async_computation.3 | async-start | bytes 1179648 | tf_op jit(solution)/shard_map/reduce_scatter | solution.py:94
  165.0 5.9 %copy-start.1 = (bf16[512,32,64]{0,2,1:T(8,128)(2,1)S(1)}, bf16[512,32,64]{0,2,1:T(8,128)(2,1)}, u32[]{:S(2)}) copy-start(bf16[512,32,64]{0,2,1:T(8,128)(2,1)} %reshape.146) | copy-start | bytes 6291460
  170.9 2.5 copy-start.2
  176.1 104.4 %all-reduce.7.cloned.1.call-start = ((), (), s32[]{:S(2)}) async-start(), calls=%async_computation.2 | async-start | bytes 4194304 | tf_op jit(solution)/shard_map/psum | solution.py:62
  177.6 3.8 %copy-start.6 = (bf16[128,2048]{0,1:T(8,128)(2,1)S(1)}, bf16[128,2048]{0,1:T(8,128)(2,1)}, u32[]{:S(2)}) copy-start(bf16[128,2048]{0,1:T(8,128)(2,1)} %copy.30) | copy-start | bytes 1572868
  187.1 10.2 %copy-start.4 = (bf16[1,128,2048]{1,2,0:T(8,128)(2,1)S(1)}, bf16[1,128,2048]{1,2,0:T(8,128)(2,1)}, u32[]{:S(2)}) copy-start(bf16[1,128,2048]{1,2,0:T(8,128)(2,1)} %copy-done.3) | copy-start | bytes 1572868
  201.6 10.2 %copy-start.5 = (bf16[128,2048]{1,0:T(8,128)(2,1)S(1)}, bf16[128,2048]{1,0:T(8,128)(2,1)}, u32[]{:S(2)}) copy-start(bf16[128,2048]{1,0:T(8,128)(2,1)} %get-tuple-element.18) | copy-start | bytes 1572868
Sparse Core Ops, SparseCore 0:
  88.2 63.2 all-reduce.4
  176.2 33.2 reduce-scatter.1
  212.6 67.7 all-reduce.6
where the time goes:
time: 292 us; the launch traced here: 291 us
  blocking collectives  107 us (37%)
  waiting for transfers between devices  65.7 us (22%)
  local copies, waits for them, and re-layouts  57.4 us (20%)
  matrix products  35.9 us (12%)
  between operations  13.9 us (5%)
  other arithmetic  10.6 us (4%)
    psum x1, waiting for transfers between devices, per_device(): lax.psum(jnp.dot(grad_rows.T, context_rows, preferred_element_type=jnp.fl...  65.7 us
    psum x1, blocking collectives, per_device(): lax.psum((jnp.sum(weights, axis=3), weighted_values(weights, value_heads)...  61.3 us
    pmax x1, blocking collectives, per_device(): row_max = lax.pmax(local_max, 'psg')  29.1 us
    unnamed x25, local copies, waits for them, and re-layouts  28.9 us
    all_gather x1, blocking collectives, per_device(): query_full = lax.all_gather(queries, 'psg', axis=2, tiled=True)  16.8 us
    another operation x2, local copies, waits for them, and re-layouts  8.74 us
    dot_general x1, matrix products, per_device(): jnp.einsum('bihe,bkhe->bhik', query_heads, key_heads, preferred_element_t...  6.12 us
    dot_general x1, matrix products, per_device(): jnp.einsum('bihe,bkhe->bhik', grad_heads, value_heads, preferred_element_...  5.91 us
  transfers between devices with their start and end apart: 3, of which 1 were waited for; matrix products, arithmetic and copies ran while one was open for 16% of the time, Pallas kernels for 0%

commit v1 on v0

--- a/solution.py
+++ b/solution.py
@@ -59,9 +59,14 @@
         jnp.bfloat16
     )
     layer_out = layer_out.reshape(question_count, answer_len, -1)
-    weight_grad = lax.psum(
-        jnp.dot(grad_rows.T, context_rows, preferred_element_type=jnp.float32).astype(jnp.bfloat16),
-        "dp",
+    weight_grad = jnp.sum(
+        lax.all_gather(
+            jnp.dot(grad_rows.T, context_rows, preferred_element_type=jnp.float32).astype(
+                jnp.bfloat16
+            ),
+            "dp",
+        ),
+        axis=0,
     ).astype(jnp.float32)
     context_grad = lax.psum(
         jnp.dot(grad_rows, out_weight, preferred_element_type=jnp.float32), "psg"

time: 292 us -> 338 us (1.16)
  waiting for transfers between devices: 65.7 us -> 82.6 us
  other arithmetic: 10.6 us -> 25.6 us
  local copies, waits for them, and re-layouts: 57.4 us -> 71.6 us
    all_gather x0 -> x1, waiting for transfers between devices: none -> 82.6 us  [per_device(): lax.all_gather(jnp.dot(grad_rows.T, context_rows, preferred_element_type=...]
    psum x1 -> x0, waiting for transfers between devices: 65.7 us -> none  [per_device(): lax.psum(jnp.dot(grad_rows.T, context_rows, preferred_element_type=jnp.fl...]
    reduce_sum x0 -> x1, other arithmetic: none -> 15 us  [per_device(): jnp.sum(lax.all_gather(jnp.dot(grad_rows.T, context_rows, preferred_eleme...]
    all_gather x0 -> x1, local copies, waits for them, and re-layouts: none -> 14.5 us  [per_device(): lax.all_gather(jnp.dot(grad_rows.T, context_rows, preferred_element_type=...]
    unnamed x25 -> x27, local copies, waits for them, and re-layouts: 28.9 us -> 28.8 us
  transfers between devices with their start and end apart: 3 -> 3, of which waited for: 1 -> 1; matrix products, arithmetic and copies ran while one was open for 16% -> 14% of each run, Pallas kernels for 0% -> 0%
where the time goes in v1:
time: 338 us; the launch traced here: 336 us
  blocking collectives  106 us (31%)
  waiting for transfers between devices  82.6 us (24%)
  local copies, waits for them, and re-layouts  71.6 us (21%)
  matrix products  36 us (11%)
  other arithmetic  25.6 us (8%)
  between operations  13.9 us (4%)
    all_gather x1, waiting for transfers between devices, per_device(): lax.all_gather(jnp.dot(grad_rows.T, context_rows, preferred_element_type=...  82.6 us
    psum x1, blocking collectives, per_device(): lax.psum((jnp.sum(weights, axis=3), weighted_values(weights, value_heads)...  60.4 us
    pmax x1, blocking collectives, per_device(): row_max = lax.pmax(local_max, 'psg')  29.1 us
    unnamed x27, local copies, waits for them, and re-layouts  28.8 us
    all_gather x1, blocking collectives, per_device(): query_full = lax.all_gather(queries, 'psg', axis=2, tiled=True)  16.5 us
    reduce_sum x1, other arithmetic, per_device(): jnp.sum(lax.all_gather(jnp.dot(grad_rows.T, context_rows, preferred_eleme...  15 us
    all_gather x1, local copies, waits for them, and re-layouts, per_device(): lax.all_gather(jnp.dot(grad_rows.T, context_rows, preferred_element_type=...  14.5 us
    another operation x2, local copies, waits for them, and re-layouts  8.74 us
  transfers between devices with their start and end apart: 3, of which 1 were waited for; matrix products, arithmetic and copies ran while one was open for 14% of the time, Pallas kernels for 0%

profile of v1, /device:TPU:0, one launch (start us, length us, event | category | flops | bytes accessed | tf_op | source)
XLA Modules:
  0.0 336.0 jit_solution(1150715187759157749)
XLA Ops:
  7.3 6.3 %copy.35 = bf16[1,2,256,2048]{2,1,3,0:T(2,128)(2,1)} copy(bf16[1,2,256,2048]{3,2,1,0:T(8,128)(2,1)} %param.7) | data formatting | bytes 4194304 | tf_op args[1]
  13.5 4.4 %reshape.146 = bf16[512,32,64]{0,2,1:T(8,128)(2,1)} reshape(bf16[1,2,256,2048]{2,1,3,0:T(2,128)(2,1)} %copy.35) | data formatting | bytes 4194304 | tf_op jit(solution)/shard_map/reshape.4
  17.9 16.5 %all_gather.9 = bf16[1,128,2048]{2,1,0:T(8,128)(2,1)S(1)} all-gather(bf16[1,128,256]{2,1,0:T(8,128)(2,1)S(1)} %copy-done.8), channel_id=1, replica_groups=mesh['dp'=4,'psg'=8] {'psg'}, dimensions={2}, use_global_device_ids=true | all-gather | bytes 589824 | tf_op jit(solution)/shard_map/all_gather | solution.py:34
  34.8 6.2 %select_reduce_fusion = (f32[32,128]{1,0:T(8,128)S(1)}, f32[32,128,512]{2,1,0:T(8,128)}) fusion(pred[512]{0:T(512)(128)(4,1)S(1)} %lt.27, bf16[128,32,64]{0,2,1:T(8,128)(2,1)S(1)} %bitcast.91, bf16[512,32,64]{0,2,1:T(8,128)(2,1)} %reshape.146), kind=kOutput, calls=%fused_computation.2 | convolution fusion | flops 272625664 | bytes 11026944 | tf_op jit(solution)/shard_map/bihe,bkhe->bhik/dot_general | solution.py:42
  41.0 29.1 %pmax.7 = f32[32,128]{1,0:T(8,128)S(1)} all-reduce(f32[32,128]{1,0:T(8,128)S(1)} %get-tuple-element.24), channel_id=1, replica_groups=mesh['dp'=4,'psg'=8] {'psg'}, use_global_device_ids=true, to_apply=%region_1.2 | all-reduce | flops 4096 | bytes 32768 | tf_op jit(solution)/shard_map/pmax | solution.py:46
  70.2 6.1 %copy.36 = bf16[1,2,256,2048]{2,1,3,0:T(2,128)(2,1)} copy(bf16[1,2,256,2048]{3,2,1,0:T(8,128)(2,1)} %param.8) | data formatting | bytes 4194304 | tf_op args[2]
  76.3 4.4 %reshape.147 = bf16[512,32,64]{0,2,1:T(8,128)(2,1)} reshape(bf16[1,2,256,2048]{2,1,3,0:T(2,128)(2,1)} %copy.36) | data formatting | bytes 4194304 | tf_op jit(solution)/shard_map/reshape.10
  80.7 5.7 %fusion.3 = f32[32,128,64]{1,2,0:T(8,128)S(1)} fusion(bf16[512,32,64]{0,2,1:T(8,128)(2,1)} %reshape.147, f32[32,128,512]{2,1,0:T(8,128)} %get-tuple-element.25, f32[32,128]{1,0:T(8,128)S(1)} %pmax.7, pred[512]{0:T(512)(128)(4,1)S(1)} %lt.27), kind=kOutput, calls=%fused_computation.6 | convolution fusion | flops 274726912 | bytes 11551232 | tf_op jit(solution)/shard_map/bhik,bkhe->bihe/dot_general | solution.py:19
  86.4 1.3 copy.37
  88.2 4.6 %fusion.1 = f32[32,128]{1,0:T(8,128)S(1)} fusion(f32[32,128,512]{2,1,0:T(8,128)} %get-tuple-element.25, f32[32,128]{1,0:T(8,128)S(1)} %pmax.7, pred[512]{0:T(512)(128)(4,1)S(1)} %lt.27), kind=kLoop, calls=%fused_computation.4 | loop fusion | flops 6287360 | bytes 8421888 | tf_op jit(solution)/shard_map/reduce_sum | solution.py:49
  92.9 60.4 %all-reduce.5 = (f32[1,32,128]{2,1,0:T(8,128)S(1)}, bf16[128,2048]{1,0:T(8,128)(2,1)}) all-reduce(f32[1,32,128]{2,1,0:T(8,128)S(1)} %bitcast.97, f32[128,2048]{1,0:T(8,128)S(1)} %fusion.17), channel_id=1, replica_groups=mesh['dp'=4,'psg'=8] {'psg'}, use_global_device_ids=true, to_apply=%region_4.5 | all-reduce | flops 266240 | bytes 1605632 | tf_op jit(solution)/shard_map/psum | solution.py:48
  153.3 2.0 copy.40
  155.4 1.3 copy.38
  156.7 3.1 convert_multiply_fusion
  159.8 2.5 copy.41
  162.3 1.3 bitcast_reduce_fusion
  163.7 5.9 %multiply_convert_fusion = bf16[32,128,512]{2,1,0:T(8,128)(2,1)S(1)} fusion(f32[32,128]{1,0:T(8,128)S(1)} %bitcast.101, bf16[128,32,64]{0,2,1:T(8,128)(2,1)} %bitcast.95, bf16[512,32,64]{0,2,1:T(8,128)(2,1)} %reshape.147, f32[32,128]{1,0:T(8,128)S(1)} %bitcast.99, f32[32,128,512]{2,1,0:T(8,128)} %get-tuple-element.25, f32[32,128]{1,0:T(8,128)S(1)} %pmax.7, ...), kind=kOutput, calls=%fused_computation | convolution fusion | flops 281018368 | bytes 15254016 | tf_op jit(solution)/shard_map/bihe,bkhe->bhik/dot_general | solution.py:80
  169.6 2.5 fusion.23
  172.1 2.5 copy.42
  176.2 3.7 %fusion.10 = bf16[512,2048]{0,1:T(8,128)(2,1)} fusion(f32[1,128,2048]{2,1,0:T(8,128)} %all-reduce.4.cloned.1.call-done, f32[1,128,2048]{2,1,0:T(8,128)} %copy.39, bf16[1,128,512]{2,1,0:T(8,128)(2,1)S(1)} %copy-done.7), kind=kOutput, calls=%fused_computation.13 | convolution fusion | flops 270008320 | bytes 4325376 | tf_op jit(solution)/shard_map/dot_general | solution.py:64
  179.9 5.8 %convert_bitcast_fusion = bf16[1,512,32,64]{1,3,2,0:T(8,128)(2,1)} fusion(bf16[128,32,64]{0,2,1:T(8,128)(2,1)S(1)} %bitcast.96, f32[32,128]{1,0:T(8,128)S(1)} %bitcast.100, f32[32,128,512]{2,1,0:T(8,128)} %get-tuple-element.25, f32[32,128]{1,0:T(8,128)S(1)} %pmax.7, pred[512]{0:T(512)(128)(4,1)S(1)} %lt.27), kind=kOutput, calls=%fused_computation.14 | convolution fusion | flops 277872640 | bytes 11043328 | tf_op jit(solution)/shard_map/bhik,bihe->bkhe/dot_general | solution.py:84
  185.7 4.0 %reshape.156 = bf16[1,2,256,2048]{2,1,3,0:T(2,128)(2,1)} reshape(bf16[1,512,32,64]{1,3,2,0:T(8,128)(2,1)} %convert_bitcast_fusion) | data formatting | bytes 4194304 | tf_op jit(solution)/shard_map/reshape | solution.py:90
  189.7 6.1 %copy.45 = bf16[1,2,256,2048]{3,2,1,0:T(8,128)(2,1)} copy(bf16[1,2,256,2048]{2,1,3,0:T(2,128)(2,1)} %reshape.156) | data formatting | bytes 4194304
  195.9 4.2 %convert_bitcast_fusion.1 = bf16[1,512,32,64]{1,3,2,0:T(8,128)(2,1)} fusion(bf16[128,32,64]{0,2,1:T(8,128)(2,1)S(1)} %bitcast.92, bf16[32,128,512]{2,1,0:T(8,128)(2,1)} %copy-done.2), kind=kOutput, calls=%fused_computation.15 | convolution fusion | flops 269484032 | bytes 6815744 | tf_op jit(solution)/shard_map/bhik,bihe->bkhe/dot_general | solution.py:91
  200.1 4.0 %reshape.155 = bf16[1,2,256,2048]{2,1,3,0:T(2,128)(2,1)} reshape(bf16[1,512,32,64]{1,3,2,0:T(8,128)(2,1)} %convert_bitcast_fusion.1) | data formatting | bytes 4194304 | tf_op jit(solution)/shard_map/reshape | solution.py:94
  204.2 6.1 %copy.44 = bf16[1,2,256,2048]{3,2,1,0:T(8,128)(2,1)} copy(bf16[1,2,256,2048]{2,1,3,0:T(2,128)(2,1)} %reshape.155) | data formatting | bytes 4194304
  210.3 1.5 fusion.14
  211.8 1.5 convert_element_type.85
  213.3 82.6 %all-gather.3.cloned.1.call-done = bf16[2048,2048]{0,1:T(8,128)(2,1)} async-done(((bf16[512,2048]{0,1:T(8,128)(2,1)}), bf16[2048,2048]{0,1:T(8,128)(2,1)}) %all-gather.3.cloned.1.call-update) | async-done | bytes 8388624 | tf_op jit(solution)/shard_map/all_gather | solution.py:63
  295.9 14.5 %reshape.158 = bf16[4,512,2048]{1,0,2:T(4,128)(2,1)} reshape(bf16[2048,2048]{0,1:T(8,128)(2,1)} %all-gather.3.cloned.1.call-done) | data formatting | bytes 16777216 | tf_op jit(solution)/shard_map/all_gather | solution.py:63
  310.4 15.0 %reduce_sum.36 = bf16[512,2048]{0,1:T(8,128)(2,1)} reduce(bf16[4,512,2048]{1,0,2:T(4,128)(2,1)} %reshape.158, bf16[]{:T(256)} %constant.5.clone.1), dimensions={0}, to_apply=%region_5.6 | reduce | flops 3145728 | bytes 10485762 | tf_op jit(solution)/shard_map/reduce_sum | solution.py:62
  325.4 4.1 %copy.43 = f32[512,2048]{1,0:T(8,128)} copy(bf16[512,2048]{0,1:T(8,128)(2,1)} %reduce_sum.36) | data formatting | bytes 6291456
  (36 shorter events, 2.6 us)
Async XLA Ops:
  7.2 80.6 %copy-start = (bf16[512,2048]{1,0:T(8,128)(2,1)S(1)}, bf16[512,2048]{1,0:T(8,128)(2,1)}, u32[]{:S(2)}) copy-start(bf16[512,2048]{1,0:T(8,128)(2,1)} %param.10) | copy-start | bytes 6291460
  7.2 149.6 %all-reduce.4.cloned.1.call-start = ((), (), s32[]{:S(2)}) async-start(), calls=%async_computation.1 | async-start | bytes 2097152 | tf_op jit(solution)/shard_map/psum | solution.py:48
  7.2 10.7 %copy-start.8 = (bf16[1,128,256]{2,1,0:T(8,128)(2,1)S(1)}, bf16[1,128,256]{2,1,0:T(8,128)(2,1)}, u32[]{:S(2)}) copy-start(bf16[1,128,256]{2,1,0:T(8,128)(2,1)} %param.6) | copy-start | bytes 196612
  7.3 27.4 %copy-start.9 = (s32[1,2]{1,0:T(1,128)S(1)}, s32[1,2]{1,0:T(1,128)}, u32[]{:S(2)}) copy-start(s32[1,2]{1,0:T(1,128)} %param.9) | copy-start | bytes 28
  34.7 6.3 %copy-start.3 = (bf16[1,128,2048]{1,2,0:T(8,128)(2,1)}, bf16[1,128,2048]{1,2,0:T(8,128)(2,1)S(1)}, u32[]{:S(2)}) copy-start(bf16[1,128,2048]{1,2,0:T(8,128)(2,1)S(1)} %copy.34) | copy-start | bytes 1572868
  80.7 7.1 %copy-start.7 = (bf16[1,128,512]{2,1,0:T(8,128)(2,1)S(1)}, bf16[1,128,512]{2,1,0:T(8,128)(2,1)}, u32[]{:S(2)}) copy-start(bf16[1,128,512]{2,1,0:T(8,128)(2,1)} %param.11) | copy-start | bytes 393220
  87.7 124.1 %reduce-scatter.2.cloned.1.call-start = ((), (), s32[]{:S(2)}) async-start(), calls=%async_computation.2 | async-start | bytes 1179648 | tf_op jit(solution)/shard_map/reduce_scatter | solution.py:99
  163.6 5.9 %copy-start.1 = (bf16[512,32,64]{0,2,1:T(8,128)(2,1)S(1)}, bf16[512,32,64]{0,2,1:T(8,128)(2,1)}, u32[]{:S(2)}) copy-start(bf16[512,32,64]{0,2,1:T(8,128)(2,1)} %reshape.146) | copy-start | bytes 6291460
  169.6 2.5 copy-start.2
  174.7 121.3 %all-gather.3.cloned.1.call-start = ((), (), s32[]{:S(2)}) async-start(), calls=%async_computation.3 | async-start | bytes 10485760 | tf_op jit(solution)/shard_map/all_gather | solution.py:63
  176.2 3.7 %copy-start.6 = (bf16[128,2048]{0,1:T(8,128)(2,1)S(1)}, bf16[128,2048]{0,1:T(8,128)(2,1)}, u32[]{:S(2)}) copy-start(bf16[128,2048]{0,1:T(8,128)(2,1)} %copy.40) | copy-start | bytes 1572868
  185.7 10.2 %copy-start.4 = (bf16[1,128,2048]{1,2,0:T(8,128)(2,1)S(1)}, bf16[1,128,2048]{1,2,0:T(8,128)(2,1)}, u32[]{:S(2)}) copy-start(bf16[1,128,2048]{1,2,0:T(8,128)(2,1)} %copy-done.3) | copy-start | bytes 1572868
  200.1 10.2 %copy-start.5 = (bf16[128,2048]{1,0:T(8,128)(2,1)S(1)}, bf16[128,2048]{1,0:T(8,128)(2,1)}, u32[]{:S(2)}) copy-start(bf16[128,2048]{1,0:T(8,128)(2,1)} %get-tuple-element.23) | copy-start | bytes 1572868
Sparse Core Ops, SparseCore 0:
  87.8 63.1 all-reduce.3
  174.8 33.7 reduce-scatter.1
  210.4 85.5 all-gather.2
